TPU v7x, 256 devices: a whole 4x4x8 slice. The times are simulated.
256 devices in a mesh: wide: 32 (over x, y, core), narrow: 8 (over z).
Axes of the slice: x: 4, y: 4, z: 8, core: 2. Of those that a mesh axis runs over, the one named last changes fastest.
Arguments:
- blocks: bfloat16 [32, 8, 16, 64, 4096], P('wide', 'narrow'), may hold values from -16 to 16
- row_tile: int32 [32, 8, 16], P('wide', 'narrow'), may hold values from 0 to 15
- col_tile: int32 [32, 8, 16], P('wide', 'narrow'), may hold values from 0 to 63, as said below
- depth_tile: int32 [32, 8, 16], P('wide', 'narrow'), may hold values from 0 to 15
- block_count: int32 [32, 8], P('wide', 'narrow'), may hold values from 4 to 16, as said below
- factor_b: bfloat16 [32768, 256], P(('wide', 'narrow')), may hold values from -40 to 40
- factor_c: bfloat16 [1024, 256], replicated, may hold values from -0.076293945 to 0.076293945
Outputs:
- a_new: float32 [32768, 256], P(('wide', 'narrow'))
- b_new: float32 [32768, 256], P(('wide', 'narrow'))
Inputs may be any that keep to these rules, and one draw needn't show every extreme that they name: `block_count`: every device holds at least 4 live blocks, and some device exactly 16. col_tile // 2 is the index of wide that holds the block's mode-2 factor rows; among the 16 slots of one device, live or not, each such index appears at most 1 times, and some index exactly 1 times.
All inputs are finite; a program needn't handle non-finite values.
Results may differ from a plain program's by a relative error of at most 0.02.
Values may be sent and summed in bfloat16 or wider, within the bound.
No kernel may reach another device: no remote copies, remote signals or barrier semaphores. Data moves between devices by JAX's collectives and lax.ppermute only.
A program may use at most 128 MiB of HBM per device.

v0:
```python
import jax
import jax.numpy as jnp
from jax import lax
from jax.sharding import PartitionSpec as P

TI_DEV = 2


def right_solve(target, matrix):
    chol_lower = jnp.linalg.cholesky(matrix)
    middle = lax.linalg.triangular_solve(
        chol_lower, target, left_side=False, lower=True, transpose_a=True
    )
    return lax.linalg.triangular_solve(
        chol_lower, middle, left_side=False, lower=True, transpose_a=False
    )


def column_gram(matrix):
    return lax.dot_general(
        matrix, matrix, (((0,), (0,)), ((), ())), preferred_element_type=jnp.float32
    )


def depth_mix(one_block, depth_id, factor_c, tile_rows):
    depth_rows = lax.dynamic_slice_in_dim(factor_c, depth_id * tile_rows, tile_rows, 0)
    depth_mixed = lax.dot_general(
        one_block, depth_rows, (((0,), (0,)), ((), ())), preferred_element_type=jnp.float32
    )
    return depth_mixed.reshape(tile_rows, tile_rows, depth_rows.shape[1])


def local(blocks, row_tile, col_tile, depth_tile, block_count, factor_b, factor_c):
    local_blocks = blocks[0, 0]
    first_ids = row_tile[0, 0]
    second_ids = col_tile[0, 0]
    depth_ids = depth_tile[0, 0]
    live_count = block_count[0, 0]
    tile_rows = local_blocks.shape[1]
    rank_width = factor_c.shape[1]
    wide_count = lax.axis_size("wide")
    narrow_count = lax.axis_size("narrow")
    second_local = factor_b.shape[0] // tile_rows
    owners = second_ids // second_local
    inside = second_ids % second_local
    gram_c = column_gram(factor_c)
    gram_b = lax.psum(column_gram(factor_b), ("wide", "narrow"))
    gathered = lax.all_gather(factor_b, "wide", axis=0, tiled=True)
    b_tiles = gathered.reshape(wide_count * second_local, tile_rows, rank_width)
    b_pick = owners * second_local + inside

    def first_step(slot_index, partial_sum):
        one_block = lax.dynamic_index_in_dim(local_blocks, slot_index, 0, False)
        depth_mixed = depth_mix(one_block, depth_ids[slot_index], factor_c, tile_rows)
        b_rows = lax.dynamic_index_in_dim(b_tiles, b_pick[slot_index], 0, False).astype(jnp.float32)
        b_term = jnp.sum(depth_mixed * b_rows[None, :, :], axis=1)
        target = first_ids[slot_index]
        current = lax.dynamic_index_in_dim(partial_sum, target, 0, False)
        return lax.dynamic_update_index_in_dim(partial_sum, current + b_term, target, 0)

    first_part = lax.fori_loop(
        0,
        live_count,
        first_step,
        jnp.zeros((narrow_count * TI_DEV, tile_rows, rank_width), jnp.float32),
    )
    mttkrp_a = lax.psum_scatter(
        first_part.reshape(-1, rank_width), "narrow", scatter_dimension=0, tiled=True
    )
    a_new = right_solve(mttkrp_a, gram_b * gram_c)
    a_half = a_new.astype(jnp.bfloat16)
    a_rows = lax.all_gather(a_half, "narrow", axis=0, tiled=True)
    gram_a = lax.psum(column_gram(a_half), ("wide", "narrow"))
    a_tiles = a_rows.reshape(a_rows.shape[0] // tile_rows, tile_rows, rank_width)
    width_slots = wide_count * second_local
    second_pick = owners * second_local + inside

    def second_step(slot_index, partial_sum):
        one_block = lax.dynamic_index_in_dim(local_blocks, slot_index, 0, False)
        depth_mixed = depth_mix(one_block, depth_ids[slot_index], factor_c, tile_rows)
        a_part = lax.dynamic_index_in_dim(a_tiles, first_ids[slot_index], 0, False).astype(
            jnp.float32
        )
        a_term = jnp.sum(depth_mixed * a_part[:, None, :], axis=0)
        target = second_pick[slot_index]
        current = lax.dynamic_index_in_dim(partial_sum, target, 0, False)
        return lax.dynamic_update_index_in_dim(partial_sum, current + a_term, target, 0)

    second_part = lax.fori_loop(
        0, live_count, second_step, jnp.zeros((width_slots, tile_rows, rank_width), jnp.float32)
    )
    mttkrp_b = lax.psum_scatter(
        second_part.reshape(-1, rank_width), "wide", scatter_dimension=0, tiled=True
    )
    b_new = right_solve(mttkrp_b, gram_a * gram_c)
    return (a_new, b_new)


def solution(mesh):
    return jax.shard_map(
        local,
        mesh=mesh,
        in_specs=(
            P("wide", "narrow", None, None, None),
            P("wide", "narrow", None),
            P("wide", "narrow", None),
            P("wide", "narrow", None),
            P("wide", "narrow"),
            P(("wide", "narrow"), None),
            P(),
        ),
        out_specs=(P(("wide", "narrow"), None), P(("wide", "narrow"), None)),
        check_vma=False,
    )
```

profile of v0, /device:TPU:2, one launch (start us, length us, event | category | flops | bytes accessed | tf_op | source)
XLA Modules:
  0.0 688.1 jit_solution(2137662635349681206)
XLA Ops:
  8.8 1.8 fusion.35
  10.8 15.6 %copy.22 = bf16[1,1,16,64,4096]{3,4,2,1,0:T(8,128)(2,1)} copy(bf16[1,1,16,64,4096]{4,3,2,1,0:T(8,128)(2,1)} %param.16) | data formatting | bytes 16777216 | tf_op args[0]
  26.4 36.2 %all-gather.2.cloned.1.call-done = bf16[4096,256]{1,0:T(8,128)(2,1)} async-done(((bf16[128,256]{1,0:T(8,128)(2,1)}), bf16[4096,256]{1,0:T(8,128)(2,1)}) %all-gather.2.cloned.1.call-update) | async-done | bytes 2097168 | tf_op jit(solution)/shard_map/all_gather | solution.py:48
  62.7 144.2 %while.28 = (s32[]{:T(128)}, f32[16,64,256]{2,1,0:T(8,128)S(1)}, s32[]{:T(128)}, s32[16]{0:T(128)S(1)}, bf16[16,64,4096]{1,2,0:T(8,128)(2,1)}, /*index=5*/s32[16...) while((s32[]{:T(128)}, f32[16,64,256]{2,1,0:T(8,128)S(1)}, ...), condition=%wide.region_7.9_spmd, body=%wide.region_5.8_spmd.sunk | while | flops 136331280 | bytes 2556253 | solution.py:61
  207.9 64.7 %all-reduce.4.cloned.1.call-done = f32[256,256]{0,1:T(8,128)} async-done(((f32[256,256]{0,1:T(8,128)}), f32[256,256]{0,1:T(8,128)}) %all-reduce.4.cloned.1.call-update) | async-done | bytes 262160 | tf_op jit(solution)/shard_map/psum | solution.py:47
  274.1 11.7 %cholesky.130 = f32[128,128]{1,0:T(8,128)S(1)} custom-call(f32[128,128]{1,0:T(8,128)S(1)} %cholesky.194), custom_call_target="Cholesky" | custom-call | tf_op jit(solution)/shard_map/jit(cholesky)/cholesky | solution.py:10
  285.9 9.8 %custom-call.17 = f32[1,128,128]{1,2,0:T(8,128)S(1)} custom-call(f32[1,128,128]{2,1,0:T(8,128)S(1)} %get-tuple-element.211), custom_call_target="InvertDiagBlocksLowerTriangular" | custom-call | tf_op jit(solution)/shard_map/jit(cholesky)/cholesky | solution.py:10
  296.2 11.7 %cholesky.147 = f32[128,128]{1,0:T(8,128)S(1)} custom-call(f32[128,128]{1,0:T(8,128)S(1)} %convolution_subtract_fusion.5), custom_call_target="Cholesky" | custom-call | tf_op jit(solution)/shard_map/jit(cholesky)/cholesky | solution.py:10
  310.0 4.2 while.30
  314.2 19.7 %custom-call.18 = f32[2,128,128]{1,2,0:T(8,128)S(1)} custom-call(f32[2,128,128]{2,1,0:T(8,128)S(1)} %get-tuple-element.131), custom_call_target="InvertDiagBlocksLowerTriangular" | custom-call | tf_op jit(solution)/shard_map/triangular_solve/custom-call.0 | solution.py:11
  337.2 24.6 %all_gather.7 = bf16[1024,256]{0,1:T(8,128)(2,1)S(1)} all-gather(bf16[128,256]{0,1:T(8,128)(2,1)S(1)} %fusion.31), channel_id=1, replica_groups=mesh['wide'=32,'narrow'=8] {'narrow'}, dimensions={0}, use_global_device_ids=true | all-gather | bytes 589824 | tf_op jit(solution)/shard_map/all_gather | solution.py:72
  362.9 2.4 broadcast_in_dim.14
  365.4 159.6 %while.29 = (s32[]{:T(128)}, f32[64,64,256]{2,1,0:T(8,128)}, s32[]{:T(128)}, s32[16]{0:T(128)S(1)}, bf16[16,64,4096]{1,2,0:T(8,128)(2,1)}, /*index=5*/s32[16]{0:...) while((s32[]{:T(128)}, f32[64,64,256]{2,1,0:T(8,128)}, ...), condition=%wide.region_12.16_spmd, body=%wide.region_10.15_spmd.sunk | while | flops 136331280 | bytes 2556253 | solution.py:89
  395.7 1.5 fusion.72
  416.9 1.5 fusion.72
  469.8 1.5 fusion.72
  480.4 1.5 fusion.72
  491.0 1.5 fusion.72
  525.7 89.8 %all-reduce.6.cloned.1.call-done = f32[256,256]{0,1:T(8,128)} async-done(((f32[256,256]{0,1:T(8,128)}), f32[256,256]{0,1:T(8,128)}) %all-reduce.6.cloned.1.call-update) | async-done | bytes 262160 | tf_op jit(solution)/shard_map/psum | solution.py:73
  616.7 11.7 %cholesky.164 = f32[128,128]{1,0:T(8,128)S(1)} custom-call(f32[128,128]{1,0:T(8,128)S(1)} %cholesky.197), custom_call_target="Cholesky" | custom-call | tf_op jit(solution)/shard_map/jit(cholesky)/cholesky | solution.py:10
  628.5 9.8 %custom-call.20 = f32[1,128,128]{1,2,0:T(8,128)S(1)} custom-call(f32[1,128,128]{2,1,0:T(8,128)S(1)} %get-tuple-element.207), custom_call_target="InvertDiagBlocksLowerTriangular" | custom-call | tf_op jit(solution)/shard_map/jit(cholesky)/cholesky | solution.py:10
  638.7 11.7 %cholesky.181 = f32[128,128]{1,0:T(8,128)S(1)} custom-call(f32[128,128]{1,0:T(8,128)S(1)} %convolution_subtract_fusion.2), custom_call_target="Cholesky" | custom-call | tf_op jit(solution)/shard_map/jit(cholesky)/cholesky | solution.py:10
  653.1 4.1 while.31
  657.3 19.7 %custom-call.21 = f32[2,128,128]{1,2,0:T(8,128)S(1)} custom-call(f32[2,128,128]{2,1,0:T(8,128)S(1)} %get-tuple-element.133), custom_call_target="InvertDiagBlocksLowerTriangular" | custom-call | tf_op jit(solution)/shard_map/triangular_solve/custom-call.0 | solution.py:11
  (287 shorter events, 166.4 us)
Async XLA Ops:
  8.0 54.6 %all-gather.2.cloned.1.call-start = ((), (), s32[]{:S(2)}) async-start(), calls=%async_computation.3 | async-start | bytes 2162688 | tf_op jit(solution)/shard_map/all_gather | solution.py:48
  8.7 263.9 %all-reduce.4.cloned.1.call-start = ((), (), s32[]{:S(2)}) async-start(), calls=%async_computation.2 | async-start | bytes 524288 | tf_op jit(solution)/shard_map/psum | solution.py:47
  10.7 323.2 %reduce-scatter.3.cloned.1.call-start = ((), (), s32[]{:S(2)}) async-start(), calls=%async_computation.4 | async-start | bytes 1179648 | tf_op jit(solution)/shard_map/reduce_scatter | solution.py:67
  10.7 15.7 %copy-start.2 = (s32[1,1,16]{2,1,0:T(1,128)S(1)}, s32[1,1,16]{2,1,0:T(1,128)}, u32[]{:S(2)}) copy-start(s32[1,1,16]{2,1,0:T(1,128)} %param.18) | copy-start | bytes 196
  10.7 51.9 %copy-start.1 = (bf16[1024,256]{1,0:T(8,128)(2,1)S(1)}, bf16[1024,256]{1,0:T(8,128)(2,1)}, u32[]{:S(2)}) copy-start(bf16[1024,256]{1,0:T(8,128)(2,1)} %param.22) | copy-start | bytes 1572868
  10.7 51.9 %copy-start.3 = (s32[1,1,16]{2,1,0:T(1,128)S(1)}, s32[1,1,16]{2,1,0:T(1,128)}, u32[]{:S(2)}) copy-start(s32[1,1,16]{2,1,0:T(1,128)} %param.17) | copy-start | bytes 196
  10.7 51.9 %copy-start.4 = (s32[1,1,16]{2,1,0:T(1,128)S(1)}, s32[1,1,16]{2,1,0:T(1,128)}, u32[]{:S(2)}) copy-start(s32[1,1,16]{2,1,0:T(1,128)} %param.19) | copy-start | bytes 196
  206.9 1.0 copy-start
  207.9 407.6 %all-reduce.6.cloned.1.call-start = ((), (), s32[]{:S(2)}) async-start(), calls=%async_computation.5 | async-start | bytes 524288 | tf_op jit(solution)/shard_map/psum | solution.py:73
  362.9 314.1 %reduce-scatter.5.cloned.1.call-start = ((), (), s32[]{:S(2)}) async-start(), calls=%async_computation.6 | async-start | bytes 4325376 | tf_op jit(solution)/shard_map/reduce_scatter | solution.py:92
Sparse Core Ops, SparseCore 0:
  11.4 51.1 all-gather.1
  208.0 42.8 reduce-scatter.2
  525.1 93.6 reduce-scatter.4
Sparse Core Ops, SparseCore 1:
  14.7 257.9 all-reduce.3
  363.0 252.5 all-reduce.5
where the time goes:
time: 694 us; the launch traced here: 688 us
  waiting for transfers between devices  191 us (28%)
  loops' own time  155 us (22%)
  other arithmetic  143 us (21%)
  local copies, waits for them, and re-layouts  121 us (17%)
  matrix products  34.1 us (5%)
  blocking collectives  24.6 us (4%)
  between operations  18.1 us (3%)
    psum x1, waiting for transfers between devices, local(): gram_a = lax.psum(column_gram(a_half), ('wide', 'narrow'))  89.8 us
    another operation x1, loops' own time, local(): lax.fori_loop(0, live_count, second_step, jnp.zeros((width_slots, tile_ro...  79.1 us
    another operation x1, loops' own time, local(): lax.fori_loop(0, live_count, first_step, jnp.zeros((narrow_count * TI_DEV...  75.7 us
    another operation x13, other arithmetic, right_solve(): chol_lower = jnp.linalg.cholesky(matrix)  68.6 us
    psum x1, waiting for transfers between devices, local(): gram_b = lax.psum(column_gram(factor_b), ('wide', 'narrow'))  64.7 us
    another operation x5, other arithmetic, right_solve(): lax.linalg.triangular_solve(chol_lower, target, left_side=False, lower=Tr...  39.4 us
    all_gather x1, waiting for transfers between devices, local(): gathered = lax.all_gather(factor_b, 'wide', axis=0, tiled=True)  36.2 us
    all_gather x1, blocking collectives, local(): a_rows = lax.all_gather(a_half, 'narrow', axis=0, tiled=True)  24.6 us
  transfers between devices with their start and end apart: 5, of which 3 were waited for; matrix products, arithmetic and copies ran while one was open for 42% of the time, Pallas kernels for 0%

commit v1 on v0

--- a/solution.py
+++ b/solution.py
@@ -44,7 +44,8 @@
     owners = second_ids // second_local
     inside = second_ids % second_local
     gram_c = column_gram(factor_c)
-    gram_b = lax.psum(column_gram(factor_b), ("wide", "narrow"))
+    vec = column_gram(factor_b)
+    gram_b = lax.psum(lax.psum(vec, "narrow"), "wide")
     gathered = lax.all_gather(factor_b, "wide", axis=0, tiled=True)
     b_tiles = gathered.reshape(wide_count * second_local, tile_rows, rank_width)
     b_pick = owners * second_local + inside

time: 694 us -> 660 us (0.951)
  waiting for transfers between devices: 191 us -> 158 us
    all_gather x1, waiting for transfers between devices: 36.2 us -> 0.03 us  [local(): gathered = lax.all_gather(factor_b, 'wide', axis=0, tiled=True)]
    psum x1, waiting for transfers between devices: 89.8 us -> 96.9 us  [local(): gram_a = lax.psum(column_gram(a_half), ('wide', 'narrow'))]
    psum x1 -> x2, waiting for transfers between devices: 64.7 us -> 60.9 us  [local(): gram_b = lax.psum(lax.psum(vec, 'narrow'), 'wide')]
  transfers between devices with their start and end apart: 5 -> 6, of which waited for: 3 -> 2; matrix products, arithmetic and copies ran while one was open for 42% -> 44% of each run, Pallas kernels for 0% -> 0%
where the time goes in v1:
time: 660 us; the launch traced here: 654 us
  waiting for transfers between devices  158 us (24%)
  loops' own time  155 us (23%)
  other arithmetic  143 us (22%)
  local copies, waits for them, and re-layouts  121 us (18%)
  matrix products  34.1 us (5%)
  blocking collectives  23.1 us (4%)
  between operations  18.4 us (3%)
    psum x1, waiting for transfers between devices, local(): gram_a = lax.psum(column_gram(a_half), ('wide', 'narrow'))  96.9 us
    another operation x1, loops' own time, local(): lax.fori_loop(0, live_count, second_step, jnp.zeros((width_slots, tile_ro...  79.1 us
    another operation x1, loops' own time, local(): lax.fori_loop(0, live_count, first_step, jnp.zeros((narrow_count * TI_DEV...  75.7 us
    another operation x13, other arithmetic, right_solve(): chol_lower = jnp.linalg.cholesky(matrix)  68.6 us
    psum x2, waiting for transfers between devices, local(): gram_b = lax.psum(lax.psum(vec, 'narrow'), 'wide')  60.9 us
    another operation x5, other arithmetic, right_solve(): lax.linalg.triangular_solve(chol_lower, target, left_side=False, lower=Tr...  39.4 us
    all_gather x1, blocking collectives, local(): a_rows = lax.all_gather(a_half, 'narrow', axis=0, tiled=True)  23.1 us
    dot_general x30, matrix products, depth_mix(): lax.dot_general(one_block, depth_rows, (((0,), (0,)), ((), ())), preferre...  22.6 us
  transfers between devices with their start and end apart: 6, of which 2 were waited for; matrix products, arithmetic and copies ran while one was open for 44% of the time, Pallas kernels for 0%

profile of v1, /device:TPU:2, one launch (start us, length us, event | category | flops | bytes accessed | tf_op | source)
XLA Modules:
  0.0 654.0 jit_solution(4381922706876876882)
XLA Ops:
  8.0 1.8 fusion.35
  10.6 15.6 %copy.22 = bf16[1,1,16,64,4096]{3,4,2,1,0:T(8,128)(2,1)} copy(bf16[1,1,16,64,4096]{4,3,2,1,0:T(8,128)(2,1)} %param.16) | data formatting | bytes 16777216 | tf_op args[0]
  26.2 60.8 %all-reduce.5.cloned.1.call-done = f32[256,256]{0,1:T(8,128)} async-done(((f32[256,256]{0,1:T(8,128)}), f32[256,256]{0,1:T(8,128)}) %all-reduce.5.cloned.1.call-update) | async-done | bytes 262160 | tf_op jit(solution)/shard_map/psum | solution.py:48
  87.3 144.1 %while.28 = (s32[]{:T(128)}, f32[16,64,256]{2,1,0:T(8,128)S(1)}, s32[]{:T(128)}, s32[16]{0:T(128)S(1)}, bf16[16,64,4096]{1,2,0:T(8,128)(2,1)}, /*index=5*/s32[16...) while((s32[]{:T(128)}, f32[16,64,256]{2,1,0:T(8,128)S(1)}, ...), condition=%wide.region_8.10_spmd, body=%wide.region_6.9_spmd.sunk | while | flops 136331280 | bytes 2556253 | solution.py:62
  234.0 11.7 %cholesky.130 = f32[128,128]{1,0:T(8,128)S(1)} custom-call(f32[128,128]{1,0:T(8,128)S(1)} %cholesky.194), custom_call_target="Cholesky" | custom-call | tf_op jit(solution)/shard_map/jit(cholesky)/cholesky | solution.py:10
  245.8 9.8 %custom-call.17 = f32[1,128,128]{1,2,0:T(8,128)S(1)} custom-call(f32[1,128,128]{2,1,0:T(8,128)S(1)} %get-tuple-element.211), custom_call_target="InvertDiagBlocksLowerTriangular" | custom-call | tf_op jit(solution)/shard_map/jit(cholesky)/cholesky | solution.py:10
  256.1 11.7 %cholesky.147 = f32[128,128]{1,0:T(8,128)S(1)} custom-call(f32[128,128]{1,0:T(8,128)S(1)} %convolution_subtract_fusion.5), custom_call_target="Cholesky" | custom-call | tf_op jit(solution)/shard_map/jit(cholesky)/cholesky | solution.py:10
  269.9 4.2 while.30
  274.1 19.7 %custom-call.18 = f32[2,128,128]{1,2,0:T(8,128)S(1)} custom-call(f32[2,128,128]{2,1,0:T(8,128)S(1)} %get-tuple-element.131), custom_call_target="InvertDiagBlocksLowerTriangular" | custom-call | tf_op jit(solution)/shard_map/triangular_solve/custom-call.0 | solution.py:11
  297.1 23.1 %all_gather.7 = bf16[1024,256]{0,1:T(8,128)(2,1)S(1)} all-gather(bf16[128,256]{0,1:T(8,128)(2,1)S(1)} %fusion.31), channel_id=1, replica_groups=mesh['wide'=32,'narrow'=8] {'narrow'}, dimensions={0}, use_global_device_ids=true | all-gather | bytes 589824 | tf_op jit(solution)/shard_map/all_gather | solution.py:73
  321.3 2.4 broadcast_in_dim.14
  323.8 159.6 %while.29 = (s32[]{:T(128)}, f32[64,64,256]{2,1,0:T(8,128)}, s32[]{:T(128)}, s32[16]{0:T(128)S(1)}, bf16[16,64,4096]{1,2,0:T(8,128)(2,1)}, /*index=5*/s32[16]{0:...) while((s32[]{:T(128)}, f32[64,64,256]{2,1,0:T(8,128)}, ...), condition=%wide.region_13.17_spmd, body=%wide.region_11.16_spmd.sunk | while | flops 136331280 | bytes 2556253 | solution.py:90
  354.1 1.5 fusion.72
  375.3 1.5 fusion.72
  417.6 1.5 fusion.72
  428.2 1.5 fusion.72
  438.8 1.5 fusion.72
  449.4 1.5 fusion.72
  484.2 96.9 %all-reduce.9.cloned.1.call-done = f32[256,256]{0,1:T(8,128)} async-done(((f32[256,256]{0,1:T(8,128)}), f32[256,256]{0,1:T(8,128)}) %all-reduce.9.cloned.1.call-update) | async-done | bytes 262160 | tf_op jit(solution)/shard_map/psum | solution.py:74
  582.3 11.7 %cholesky.164 = f32[128,128]{1,0:T(8,128)S(1)} custom-call(f32[128,128]{1,0:T(8,128)S(1)} %cholesky.197), custom_call_target="Cholesky" | custom-call | tf_op jit(solution)/shard_map/jit(cholesky)/cholesky | solution.py:10
  594.0 9.8 %custom-call.20 = f32[1,128,128]{1,2,0:T(8,128)S(1)} custom-call(f32[1,128,128]{2,1,0:T(8,128)S(1)} %get-tuple-element.207), custom_call_target="InvertDiagBlocksLowerTriangular" | custom-call | tf_op jit(solution)/shard_map/jit(cholesky)/cholesky | solution.py:10
  604.3 11.7 %cholesky.181 = f32[128,128]{1,0:T(8,128)S(1)} custom-call(f32[128,128]{1,0:T(8,128)S(1)} %convolution_subtract_fusion.2), custom_call_target="Cholesky" | custom-call | tf_op jit(solution)/shard_map/jit(cholesky)/cholesky | solution.py:10
  618.7 4.1 while.31
  622.9 19.7 %custom-call.21 = f32[2,128,128]{1,2,0:T(8,128)S(1)} custom-call(f32[2,128,128]{2,1,0:T(8,128)S(1)} %get-tuple-element.133), custom_call_target="InvertDiagBlocksLowerTriangular" | custom-call | tf_op jit(solution)/shard_map/triangular_solve/custom-call.0 | solution.py:11
  (290 shorter events, 164.8 us)
Async XLA Ops:
  8.0 79.1 %all-reduce.5.cloned.1.call-start = ((), (), s32[]{:S(2)}) async-start(), calls=%async_computation.2 | async-start | bytes 524288 | tf_op jit(solution)/shard_map/psum | solution.py:48
  9.9 77.3 %all-gather.2.cloned.1.call-start = ((), (), s32[]{:S(2)}) async-start(), calls=%async_computation.4 | async-start | bytes 2162688 | tf_op jit(solution)/shard_map/all_gather | solution.py:49
  10.5 222.0 %all-reduce.7.cloned.1.call-start = ((), (), s32[]{:S(2)}) async-start(), calls=%async_computation.3 | async-start | bytes 524288 | tf_op jit(solution)/shard_map/psum | solution.py:48
  10.5 15.7 %copy-start.2 = (s32[1,1,16]{2,1,0:T(1,128)S(1)}, s32[1,1,16]{2,1,0:T(1,128)}, u32[]{:S(2)}) copy-start(s32[1,1,16]{2,1,0:T(1,128)} %param.18) | copy-start | bytes 196
  10.6 76.7 %copy-start.1 = (bf16[1024,256]{1,0:T(8,128)(2,1)S(1)}, bf16[1024,256]{1,0:T(8,128)(2,1)}, u32[]{:S(2)}) copy-start(bf16[1024,256]{1,0:T(8,128)(2,1)} %param.22) | copy-start | bytes 1572868
  10.6 76.7 %copy-start.3 = (s32[1,1,16]{2,1,0:T(1,128)S(1)}, s32[1,1,16]{2,1,0:T(1,128)}, u32[]{:S(2)}) copy-start(s32[1,1,16]{2,1,0:T(1,128)} %param.17) | copy-start | bytes 196
  10.6 76.7 %copy-start.4 = (s32[1,1,16]{2,1,0:T(1,128)S(1)}, s32[1,1,16]{2,1,0:T(1,128)}, u32[]{:S(2)}) copy-start(s32[1,1,16]{2,1,0:T(1,128)} %param.19) | copy-start | bytes 196
  87.1 206.7 %reduce-scatter.3.cloned.1.call-start = ((), (), s32[]{:S(2)}) async-start(), calls=%async_computation.5 | async-start | bytes 1179648 | tf_op jit(solution)/shard_map/reduce_scatter | solution.py:68
  231.4 1.0 copy-start
  232.4 348.6 %all-reduce.9.cloned.1.call-start = ((), (), s32[]{:S(2)}) async-start(), calls=%async_computation.6 | async-start | bytes 524288 | tf_op jit(solution)/shard_map/psum | solution.py:74
  321.3 321.3 %reduce-scatter.5.cloned.1.call-start = ((), (), s32[]{:S(2)}) async-start(), calls=%async_computation.7 | async-start | bytes 4325376 | tf_op jit(solution)/shard_map/reduce_scatter | solution.py:93
Sparse Core Ops, SparseCore 0:
  11.1 75.9 all-reduce.4
  232.6 44.1 reduce-scatter.2
  321.4 259.6 all-reduce.8
Sparse Core Ops, SparseCore 1:
  12.9 51.1 all-gather.1
  87.2 110.0 all-reduce.6
  483.5 104.6 reduce-scatter.4
